TPU v7x, 32 devices: a whole 2x2x4 slice. The times are simulated.
32 devices in a mesh: parts: 2 (over y), cell: 4 (over z), grp: 4 (over x, core).
Axes of the slice: x: 2, y: 2, z: 4, core: 2. Of those that a mesh axis runs over, the one named last changes fastest.
Arguments:
- sketch: bfloat16 [98304, 256], P(('parts', 'cell', 'grp')), parts along dimension 0, may hold values from -0.27063294 to 0.27063294, as said below
- slab: bfloat16 [98304, 128], P(('parts', 'cell', 'grp')), parts along dimension 0, may hold values from -6 to 6
Outputs:
- r_factor: float32 [512, 256], P('parts'), parts along dimension 0
- basis: bfloat16 [98304, 256], P(('parts', 'cell', 'grp')), parts along dimension 0
- projected: float32 [512, 128], P(('parts', 'cell'), 'grp'), parts along dimension 0
There are 2 independent parts, one for each index of `parts`. A program takes and returns all parts, laid end to end along the dimension named above; each array names one. Nothing has to cross between parts.
Inputs may be any that keep to these rules, and one draw needn't show every extreme that they name: A scaled random sketch of full column rank.
All inputs are finite; a program needn't handle non-finite values.
Results may differ from a plain program's by a relative error of at most 0.001.
Values sent between devices are 32-bit elements; how exact they have to be, the bound alone decides.
A program may use at most 64 MiB of HBM per device.

v0:
```python
import jax
import jax.numpy as jnp
from jax import lax
from jax.sharding import PartitionSpec as P


def gram_of(piece):
    return lax.dot_general(
        piece, piece, (((0,), (0,)), ((), ())), preferred_element_type=jnp.float32
    )


def local(sketch, slab):
    own_gram = gram_of(sketch)
    own_cross = lax.dot_general(
        sketch, slab, (((0,), (0,)), ((), ())), preferred_element_type=jnp.float32
    )
    total_gram, total_cross = lax.psum((own_gram, own_cross), ("cell", "grp"))
    lower_factor = jnp.linalg.cholesky(total_gram)
    whole_proj = lax.linalg.triangular_solve(lower_factor, total_cross, left_side=True, lower=True)
    row_count = whole_proj.shape[0] // lax.axis_size("cell")
    col_count = whole_proj.shape[1] // lax.axis_size("grp")
    row_start = lax.axis_index("cell") * row_count
    col_start = lax.axis_index("grp") * col_count
    projected = lax.dynamic_slice(whole_proj, (row_start, col_start), (row_count, col_count))
    identity = jnp.eye(lower_factor.shape[0], dtype=jnp.float32)
    inverse_lower = lax.linalg.triangular_solve(lower_factor, identity, left_side=True, lower=True)
    exact_rows = jnp.dot(
        sketch.astype(jnp.float32),
        inverse_lower.T,
        precision=lax.Precision.HIGHEST,
        preferred_element_type=jnp.float32,
    )
    basis = exact_rows.astype(jnp.bfloat16)
    return (lower_factor.T, basis, projected)


def solution(mesh):
    in_specs = (P(("parts", "cell", "grp"), None), P(("parts", "cell", "grp"), None))
    out_specs = (P("parts", None), P(("parts", "cell", "grp"), None), P(("parts", "cell"), "grp"))
    return jax.shard_map(local, mesh=mesh, in_specs=in_specs, out_specs=out_specs, check_vma=False)
```

profile of v0, /device:TPU:0, one launch (start us, length us, event | category | flops | bytes accessed | tf_op | source)
XLA Modules:
  0.0 181.2 jit_solution(13206856936610016307)
XLA Ops:
  7.2 0.0 copy-start
  7.2 0.0 copy-start.1
  7.2 0.0 all-reduce.4.cloned.1.call-start
  7.2 1.3 copy-done
  8.6 1.4 fusion.21
  10.0 0.0 copy-done.1
  10.0 1.3 fusion.22
  11.3 0.0 all-reduce.4.cloned.1.call-update
  11.4 95.0 %all-reduce.4.cloned.1.call-done = (f32[256,256]{0,1:T(8,128)}, f32[256,128]{1,0:T(8,128)}) async-done(((f32[256,256]{0,1:T(8,128)}, f32[256,128]{1,0:T(8,128)}), (f32[256,256]{0,1:T(8,128)}, f32[256,128]{1,0:T(8,128)})) %all-reduce.4.cloned.1.call-update) | async-done | bytes 393232 | tf_op jit(solution)/shard_map/psum | solution.py:18
  106.4 1.1 copy.6
  107.4 1.0 fusion.4
  108.5 11.7 %cholesky.50 = f32[128,128]{1,0:T(8,128)S(1)} custom-call(f32[128,128]{1,0:T(8,128)S(1)} %cholesky.118), custom_call_target="Cholesky" | custom-call | tf_op jit(solution)/shard_map/jit(cholesky)/cholesky | solution.py:19
  120.2 9.8 %custom-call.16 = f32[1,128,128]{1,2,0:T(8,128)S(1)} custom-call(f32[1,128,128]{2,1,0:T(8,128)S(1)} %get-tuple-element.31), custom_call_target="InvertDiagBlocksLowerTriangular" | custom-call | tf_op jit(solution)/shard_map/jit(cholesky)/cholesky | solution.py:19
  130.0 0.0 copy-start.2
  130.1 0.2 constant_dynamic-update-slice_fusion.1
  130.3 0.3 convolution_subtract_fusion.2
  130.5 11.7 %cholesky.105 = f32[128,128]{1,0:T(8,128)S(1)} custom-call(f32[128,128]{1,0:T(8,128)S(1)} %convolution_subtract_fusion.2), custom_call_target="Cholesky" | custom-call | tf_op jit(solution)/shard_map/jit(cholesky)/cholesky | solution.py:19
  142.3 0.6 compare_reduce_fusion
  144.3 0.8 copy.7
  145.1 0.1 triangular_solve.59
  145.2 4.0 %while.1 = (s32[]{:T(128)}, f32[256,256]{1,0:T(8,128)S(1)}, s32[2,2]{1,0:T(2,128)S(1)}, f32[2,128,128]{2,1,0:T(8,128)S(1)}, s32[]{:T(128)}) while((s32[]{:T(128)}, f32[256,256]{1,0:T(8,128)S(1)}, s32[2,2]{1,0:T(2,128)S(1)}, f32[2,128,128]{2,1,0:T(8,128)S(1)}, s32[]{:T(128)}) %tuple.29), condition=%wide.while_cond, body=%wide.while_body.sunk | while | flops 2 | bytes 131189 | solution.py:27
  145.2 0.6 fusion.35
  145.8 1.4 bitcast_dynamic-update-slice_fusion.2
  147.2 0.6 fusion.35
  147.8 1.4 bitcast_dynamic-update-slice_fusion.2
  149.2 19.7 %custom-call.17 = f32[2,128,128]{1,2,0:T(8,128)S(1)} custom-call(f32[2,128,128]{2,1,0:T(8,128)S(1)} %get-tuple-element.10), custom_call_target="InvertDiagBlocksLowerTriangular" | custom-call | tf_op jit(solution)/shard_map/triangular_solve | solution.py:27
  168.9 0.0 copy-done.2
  168.9 0.3 fusion.9
  169.2 0.2 convolution_subtract_fusion.1
  169.4 0.3 fusion.14
  169.7 0.1 fusion.18
  169.8 0.7 copy.9
  170.5 0.3 fusion.7
  170.7 0.3 convolution_subtract_fusion
  171.0 0.3 fusion.15
  171.3 1.4 fusion
  172.7 1.6 copy.8
  (10 shorter events, 0.2 us)
Async XLA Ops:
  7.2 1.4 copy-start
  7.2 2.8 %copy-start.1 = (bf16[3072,128]{1,0:T(8,128)(2,1)S(1)}, bf16[3072,128]{1,0:T(8,128)(2,1)}, u32[]{:S(2)}) copy-start(bf16[3072,128]{1,0:T(8,128)(2,1)} %param.3) | copy-start | bytes 2359300
  7.2 99.2 %all-reduce.4.cloned.1.call-start = ((), (), s32[]{:S(2)}) async-start(), calls=%async_computation | async-start | bytes 786432 | tf_op jit(solution)/shard_map/psum | solution.py:18
  130.0 38.8 %copy-start.2 = (f32[256,128]{1,0:T(8,128)S(1)}, f32[256,128]{1,0:T(8,128)}, u32[]{:S(2)}) copy-start(f32[256,128]{1,0:T(8,128)} %get-tuple-element.23) | copy-start | bytes 393220
Sparse Core Ops, SparseCore 0:
  12.0 94.2 all-reduce.3
where the time goes:
time: 181 us
  waiting for transfers between devices  95 us (52%)
  other arithmetic  54.8 us (30%)
  between operations  15.5 us (9%)
  local copies, waits for them, and re-layouts  9.57 us (5%)
  matrix products  6.21 us (3%)
    psum x1, waiting for transfers between devices, local(): total_gram, total_cross = lax.psum((own_gram, own_cross), ('cell', 'grp'))  95 us
    another operation x6, other arithmetic, local(): lower_factor = jnp.linalg.cholesky(total_gram)  34 us
    another operation x3, other arithmetic, local(): lax.linalg.triangular_solve(lower_factor, identity, left_side=True, lower...  19.7 us
    unnamed x9, local copies, waits for them, and re-layouts  4.44 us
    another operation x6, local copies, waits for them, and re-layouts  3.95 us
  transfers between devices with their start and end apart: 1, of which 1 were waited for; matrix products, arithmetic and copies ran while one was open for 0% of the time, Pallas kernels for 0%

commit v1 on v0

v1 whole, which is shorter than its diff:
```python
import functools

import jax
import jax.numpy as jnp
from jax import lax
from jax.experimental import pallas as pl
from jax.experimental.pallas import tpu as pltpu
from jax.sharding import PartitionSpec as P

SUB = 8
HIGHEST = lax.Precision.HIGHEST


def dot(a, b, contract, precision=None):
    return lax.dot_general(
        a, b, (contract, ((), ())), precision=precision, preferred_element_type=jnp.float32
    )


def sums_over(a_ref, b_ref, step):
    total = None
    for start in range(0, a_ref.shape[0], step):
        rows = pl.ds(start, min(step, a_ref.shape[0] - start))
        part = dot(a_ref[rows, :], b_ref[rows, :], ((0,), (0,)))
        total = part if total is None else total + part
    return total


def reduce_kernel(
    cells, grps, sketch_ref, slab_ref, gram_ref, cross_ref,
    own_gram, own_cross, grp_gram, grp_cross, cell_gram, cell_cross,
    gs_send, gs_recv, cs_send, cs_recv, gz_send, gz_recv, cz_send, cz_recv, ag_send, ag_recv,
):
    me_c = lax.axis_index("cell")
    me_g = lax.axis_index("grp")
    half = own_gram.shape[1]
    gram_rows = own_gram.shape[0] // grps
    cross_rows = own_cross.shape[0] // grps
    days = cross_rows // 2

    barrier = pltpu.get_barrier_semaphore()
    for d in range(1, grps):
        pl.semaphore_signal(barrier, inc=1, device_id={"grp": lax.rem(me_g + d, grps)}, device_id_type=pl.DeviceIdType.MESH)
    for d in range(1, cells):
        pl.semaphore_signal(barrier, inc=1, device_id={"cell": lax.rem(me_c + d, cells)}, device_id_type=pl.DeviceIdType.MESH)

    gram = sums_over(sketch_ref, sketch_ref, 1024)
    own_gram[0:half, :] = gram[:half, :half]
    own_gram[half : 2 * half, :] = gram[:half, half:]
    own_gram[2 * half :, :] = gram[half:, half:]
    pl.semaphore_wait(barrier, grps + cells - 2)

    def rows_of(ref, index, count):
        return ref.at[pl.ds(pl.multiple_of(index * count, SUB), count), :]

    def to_grps(own, landing, count, send, recv):
        copies = []
        for d in range(1, grps):
            peer = lax.rem(me_g + d, grps)
            copies.append(pltpu.make_async_remote_copy(
                src_ref=rows_of(own, peer, count), dst_ref=landing.at[d - 1],
                send_sem=send.at[d - 1], recv_sem=recv.at[d - 1],
                device_id={"grp": peer}, device_id_type=pl.DeviceIdType.MESH))
        for copy in copies:
            copy.start()
        return copies

    def to_cells(slots, send, recv):
        copies = []
        for d in range(1, cells):
            peer = lax.rem(me_c + d, cells)
            copies.append(pltpu.make_async_remote_copy(
                src_ref=slots.at[me_c], dst_ref=slots.at[me_c],
                send_sem=send.at[d - 1], recv_sem=recv.at[d - 1],
                device_id={"cell": peer}, device_id_type=pl.DeviceIdType.MESH))
        for copy in copies:
            copy.start()
        return copies

    gs = to_grps(own_gram, grp_gram, gram_rows, gs_send, gs_recv)

    cross = sums_over(slab_ref, sketch_ref, 1024)
    for g in range(grps):
        own_cross[g * cross_rows : g * cross_rows + days, :] = cross[g * days : (g + 1) * days, :half]
        own_cross[g * cross_rows + days : (g + 1) * cross_rows, :] = cross[g * days : (g + 1) * days, half:]
    cs = to_grps(own_cross, grp_cross, cross_rows, cs_send, cs_recv)

    def sum_grps(copies, own, landing, count, slots):
        for copy in copies:
            copy.wait_recv()
        total = own[pl.ds(pl.multiple_of(me_g * count, SUB), count), :]
        for d in range(1, grps):
            total = total + landing[d - 1]
        slots[me_c] = total

    sum_grps(gs, own_gram, grp_gram, gram_rows, cell_gram)
    gz = to_cells(cell_gram, gz_send, gz_recv)
    sum_grps(cs, own_cross, grp_cross, cross_rows, cell_cross)
    cz = to_cells(cell_cross, cz_send, cz_recv)

    def sum_cells(copies, slots):
        for copy in copies:
            copy.wait_recv()
        total = slots[0]
        for c in range(1, cells):
            total = total + slots[c]
        return total

    gram_ref[pl.ds(pl.multiple_of(me_g * gram_rows, SUB), gram_rows), :] = sum_cells(gz, cell_gram)
    ag = []
    for d in range(1, grps):
        own = rows_of(gram_ref, me_g, gram_rows)
        ag.append(pltpu.make_async_remote_copy(
            src_ref=own, dst_ref=own, send_sem=ag_send.at[d - 1], recv_sem=ag_recv.at[d - 1],
            device_id={"grp": lax.rem(me_g + d, grps)}, device_id_type=pl.DeviceIdType.MESH))
    for copy in ag:
        copy.start()
    cross_ref[...] = sum_cells(cz, cell_cross)
    for copy in ag:
        copy.wait_recv()
    for copy in gs + cs + gz + cz + ag:
        copy.wait_send()


def reduced(sketch, slab, cells, grps):
    k, days = sketch.shape[1], slab.shape[1]
    half = k // 2
    gram_rows, cross_rows = 3 * half // grps, 2 * days // grps
    if gram_rows % SUB or cross_rows % (2 * SUB) or 3 * half % grps or grps < 2 or cells < 2:
        gram, cross = lax.psum((dot(sketch, sketch, ((0,), (0,))), dot(slab, sketch, ((0,), (0,)))), ("cell", "grp"))
        blocks = jnp.concatenate([gram[:half, :half], gram[:half, half:], gram[half:, half:]], axis=0)
        width = days // grps
        mine = lax.dynamic_slice(cross, (lax.axis_index("grp") * width, 0), (width, k))
        return blocks, jnp.concatenate([mine[:, :half], mine[:, half:]], axis=0)
    f32 = jnp.float32
    dma = pltpu.SemaphoreType.DMA
    return pl.pallas_call(
        functools.partial(reduce_kernel, cells, grps),
        out_shape=(jax.ShapeDtypeStruct((3 * half, half), f32), jax.ShapeDtypeStruct((cross_rows, half), f32)),
        in_specs=[pl.BlockSpec(memory_space=pltpu.VMEM)] * 2,
        out_specs=(pl.BlockSpec(memory_space=pltpu.VMEM),) * 2,
        scratch_shapes=[
            pltpu.VMEM((3 * half, half), f32),
            pltpu.VMEM((2 * days, half), f32),
            pltpu.VMEM((grps - 1, gram_rows, half), f32),
            pltpu.VMEM((grps - 1, cross_rows, half), f32),
            pltpu.VMEM((cells, gram_rows, half), f32),
            pltpu.VMEM((cells, cross_rows, half), f32),
        ] + [dma((grps - 1,))] * 4 + [dma((cells - 1,))] * 4 + [dma((grps - 1,))] * 2,
        compiler_params=pltpu.CompilerParams(collective_id=0, has_side_effects=True),
        name="reduce_sums",
    )(sketch, slab)


def factor(block):
    n = block.shape[0]
    shape = (SUB, n)
    tiles = n // SUB
    sub = lax.broadcasted_iota(jnp.int32, shape, 0)
    lane = lax.broadcasted_iota(jnp.int32, shape, 1)
    m = [block[q * SUB : (q + 1) * SUB, :] for q in range(tiles)]
    w = [jnp.where(lane == sub + q * SUB, 1.0, 0.0).astype(jnp.float32) for q in range(tiles)]
    upper, inverse = [], []

    def row(x, j):
        return jnp.broadcast_to(x[j : j + 1, :], shape)

    def col(x, j):
        return jnp.broadcast_to(x[:, j : j + 1], shape)

    for p in range(tiles):
        t, v = m[p], w[p]
        c = [col(t, p * SUB + i) for i in range(SUB)]
        r_t, r_v = jnp.zeros(shape, jnp.float32), jnp.zeros(shape, jnp.float32)
        for j in range(SUB):
            at = sub == j
            pivot = row(c[j], j)
            inv, root = 1.0 / pivot, lax.rsqrt(pivot)
            f = jnp.where(at, -inv, c[j] * inv)
            t_j, v_j = row(t, j), row(v, j)
            r_t = jnp.where(at, t_j * root, r_t)
            r_v = jnp.where(at, v_j * root, r_v)
            t = jnp.where(at, 0.0, t) - f * t_j
            v = jnp.where(at, 0.0, v) - f * v_j
            for i in range(j + 1, SUB):
                c[i] = jnp.where(at, 0.0, c[i]) - f * row(c[i], j)
        upper.append(jnp.where(lane >= sub + p * SUB, r_t, 0.0))
        inverse.append(r_v)
        if p + 1 < tiles:
            t_rows = [row(t, i) for i in range(SUB)]
            v_rows = [row(v, i) for i in range(SUB)]
            for q in range(p + 1, tiles):
                old = m[q]
                new, new_w = old, w[q]
                for i in range(SUB):
                    c_i = col(old, p * SUB + i)
                    new = new - c_i * t_rows[i]
                    new_w = new_w - c_i * v_rows[i]
                m[q], w[q] = new, new_w
    return jnp.concatenate(upper, axis=0), jnp.concatenate(inverse, axis=0)


def factor_kernel(gram_ref, cross_ref, sketch_ref, r_ref, basis_ref, proj_ref, inv_ref):
    half = gram_ref.shape[1]
    days = cross_ref.shape[0] // 2
    r11, w11 = factor(gram_ref[0:half, :])
    r12 = dot(w11, gram_ref[half : 2 * half, :], ((1,), (0,)), HIGHEST)
    r21 = r12.T
    rest = gram_ref[2 * half :, :] - dot(r21, r12, ((1,), (0,)), HIGHEST)
    mixed = dot(r21, w11, ((1,), (0,)), HIGHEST)
    r22, w22 = factor(rest)
    w21 = -dot(w22, mixed, ((1,), (0,)), HIGHEST)
    zero = jnp.zeros((half, half), jnp.float32)
    r_ref[0:half, 0:half] = r11
    r_ref[0:half, half:] = r12
    r_ref[half:, 0:half] = zero
    r_ref[half:, half:] = r22
    inv_ref[0:half, 0:half] = w11
    inv_ref[0:half, half:] = zero
    inv_ref[half:, 0:half] = w21
    inv_ref[half:, half:] = w22
    rows = proj_ref.shape[0]
    mine = inv_ref[pl.ds(pl.multiple_of(lax.axis_index("cell") * rows, SUB), rows), :]
    proj_ref[...] = dot(mine[:, :half], cross_ref[0:days, :], ((1,), (1,)), HIGHEST) + dot(
        mine[:, half:], cross_ref[days:, :], ((1,), (1,)), HIGHEST)
    whole = inv_ref[...]
    high = whole.astype(jnp.bfloat16)
    low = (whole - high.astype(jnp.float32)).astype(jnp.bfloat16)
    total = sketch_ref.shape[0]
    step = min(512, total)

    for start in range(0, total, step):
        part = sketch_ref[start : start + step, :]
        exact = dot(part, high, ((1,), (1,))) + dot(part, low, ((1,), (1,)))
        basis_ref[start : start + step, :] = exact.astype(jnp.bfloat16)


def local(cells, grps, sketch, slab):
    k, days = sketch.shape[1], slab.shape[1]
    blocks, cross = reduced(sketch, slab, cells, grps)
    vmem = pl.BlockSpec(memory_space=pltpu.VMEM)
    return pl.pallas_call(
        factor_kernel,
        out_shape=(
            jax.ShapeDtypeStruct((k, k), jnp.float32),
            jax.ShapeDtypeStruct(sketch.shape, jnp.bfloat16),
            jax.ShapeDtypeStruct((k // cells, days // grps), jnp.float32),
        ),
        in_specs=[vmem] * 3,
        out_specs=(vmem,) * 3,
        scratch_shapes=[pltpu.VMEM((k, k), jnp.float32)],
        name="factor_and_basis",
    )(blocks, cross, sketch)


def solution(mesh):
    cells, grps = mesh.shape["cell"], mesh.shape["grp"]
    in_specs = (P(("parts", "cell", "grp"), None), P(("parts", "cell", "grp"), None))
    out_specs = (P("parts", None), P(("parts", "cell", "grp"), None), P(("parts", "cell"), "grp"))
    return jax.shard_map(
        functools.partial(local, cells, grps), mesh=mesh, in_specs=in_specs, out_specs=out_specs, check_vma=False)
```

time: 181 us -> 36.4 us (0.20)
  waiting for transfers between devices: 95 us -> 0 us
  other arithmetic: 54.8 us -> 0 us
  Pallas kernels: 0 us -> 34.1 us
  between operations: 15.5 us -> 0.64 us
  local copies, waits for them, and re-layouts: 9.57 us -> 1.44 us
  matrix products: 6.21 us -> 0 us
    psum x1 -> x0, waiting for transfers between devices: 95 us -> none  [local(): total_gram, total_cross = lax.psum((own_gram, own_cross), ('cell', 'grp'))]
    another operation x10 -> x0, other arithmetic: 53.8 us -> none  [the longest x6 34 us: local(): lower_factor = jnp.linalg.cholesky(total_gram)]
    pallas_call x0 -> x2, Pallas kernels: none -> 34.1 us  [the longest x1 20.2 us: reduced(): pl.pallas_call(functools.partial(reduce_kernel, cells, grps), out_shape=(...]
    unnamed x9 -> x0, local copies, waits for them, and re-layouts: 4.44 us -> none
    dot_general x3 -> x0, matrix products: 4.13 us -> none  [the longest x1 1.43 us: local(): jnp.dot(sketch.astype(jnp.float32), inverse_lower.T, precision=lax.Precis...]
    another operation x9 -> x0, local copies, waits for them, and re-layouts: 4.05 us -> none
    another operation x8 -> x0, matrix products: 2.08 us -> none  [the longest x3 0.83 us: local(): lax.linalg.triangular_solve(lower_factor, identity, left_side=True, lower...]
  transfers between devices with their start and end apart: 1 -> 0, of which waited for: 1 -> 0; matrix products, arithmetic and copies ran while one was open for 0% -> 0% of each run, Pallas kernels for 0% -> 0%
where the time goes in v1:
time: 36.4 us; the launch traced here: 36.2 us
  Pallas kernels  34.1 us (94%)
  local copies, waits for them, and re-layouts  1.44 us (4%)
  between operations  0.64 us (2%)
    pallas_call x1, Pallas kernels, reduced(): pl.pallas_call(functools.partial(reduce_kernel, cells, grps), out_shape=(...  20.2 us
    pallas_call x1, Pallas kernels, local(): pl.pallas_call(factor_kernel, out_shape=(jax.ShapeDtypeStruct((k, k), jnp...  13.9 us
    pallas_call x1, local copies, waits for them, and re-layouts, local(): pl.pallas_call(factor_kernel, out_shape=(jax.ShapeDtypeStruct((k, k), jnp...  1.44 us

profile of v1, /device:TPU:0, one launch (start us, length us, event | category | flops | bytes accessed | tf_op | source)
XLA Modules:
  0.0 36.2 jit_solution(14193553866336966495)
XLA Ops:
  0.6 20.2 %reduce_sums.1 = (f32[384,128]{1,0:T(8,128)}, f32[64,128]{1,0:T(8,128)}) custom-call(bf16[3072,256]{1,0:T(8,128)(2,1)} %sketch_ref.3, bf16[3072,128]{1,0:T(8,128)(2,1)} %slab_ref.1), custom_call_target="tpu_custom_call" | custom-call | tf_op jit(solution)/shard_map/reduce_sums/pallas_call | solution.py:137
  20.9 13.9 %factor_and_basis.1 = (f32[256,256]{1,0:T(8,128)}, bf16[3072,256]{1,0:T(8,128)(2,1)}, f32[64,32]{1,0:T(8,128)}) custom-call(f32[384,128]{1,0:T(8,128)} %get-tuple-element.5.gram_ref, f32[64,128]{1,0:T(8,128)} %get-tuple-element.6.cross_ref, bf16[3072,256]{1,0:T(8,128)(2,1)} %sketch_ref.3), custom_call_target="tpu_custom_call" | custom-call | tf_op jit(solution)/shard_map/factor_and_basis/pallas_call | solution.py:242
  34.7 1.4 %copy.5 = f32[64,32]{0,1:T(8,128)} copy(f32[64,32]{1,0:T(8,128)} %get-tuple-element.9) | data formatting | bytes 16384 | tf_op jit(solution)/shard_map/factor_and_basis/pallas_call | solution.py:242

commit v2 on v1

--- a/solution.py
+++ b/solution.py
@@ -8,6 +8,8 @@
 from jax.sharding import PartitionSpec as P
 
 SUB = 8
+SUM_STEP = 768
+BASIS_STEP = 512
 HIGHEST = lax.Precision.HIGHEST
 
 
@@ -17,20 +19,35 @@
     )
 
 
-def sums_over(a_ref, b_ref, step):
+def chunks_of(total, step):
+    return [pl.ds(start, min(step, total - start)) for start in range(0, total, step)]
+
+
+def sums_over(a_ref, b_ref, loads):
     total = None
-    for start in range(0, a_ref.shape[0], step):
-        rows = pl.ds(start, min(step, a_ref.shape[0] - start))
+    for rows, load in loads:
+        load.wait()
         part = dot(a_ref[rows, :], b_ref[rows, :], ((0,), (0,)))
         total = part if total is None else total + part
     return total
 
 
 def reduce_kernel(
-    cells, grps, sketch_ref, slab_ref, gram_ref, cross_ref,
+    cells, grps, sketch_hbm, slab_hbm, gram_ref, cross_ref,
+    sketch_ref, slab_ref, sketch_sems, slab_sems,
     own_gram, own_cross, grp_gram, grp_cross, cell_gram, cell_cross,
     gs_send, gs_recv, cs_send, cs_recv, gz_send, gz_recv, cz_send, cz_recv, ag_send, ag_recv,
 ):
+    def loading(source, target, sems):
+        loads = []
+        for i, rows in enumerate(chunks_of(source.shape[0], SUM_STEP)):
+            load = pltpu.make_async_copy(source.at[rows, :], target.at[rows, :], sems.at[i])
+            load.start()
+            loads.append((rows, load))
+        return loads
+
+    sketch_loads = loading(sketch_hbm, sketch_ref, sketch_sems)
+    slab_loads = loading(slab_hbm, slab_ref, slab_sems)
     me_c = lax.axis_index("cell")
     me_g = lax.axis_index("grp")
     half = own_gram.shape[1]
@@ -44,7 +61,7 @@
     for d in range(1, cells):
         pl.semaphore_signal(barrier, inc=1, device_id={"cell": lax.rem(me_c + d, cells)}, device_id_type=pl.DeviceIdType.MESH)
 
-    gram = sums_over(sketch_ref, sketch_ref, 1024)
+    gram = sums_over(sketch_ref, sketch_ref, sketch_loads)
     own_gram[0:half, :] = gram[:half, :half]
     own_gram[half : 2 * half, :] = gram[:half, half:]
     own_gram[2 * half :, :] = gram[half:, half:]
@@ -79,7 +96,7 @@
 
     gs = to_grps(own_gram, grp_gram, gram_rows, gs_send, gs_recv)
 
-    cross = sums_over(slab_ref, sketch_ref, 1024)
+    cross = sums_over(slab_ref, sketch_ref, slab_loads)
     for g in range(grps):
         own_cross[g * cross_rows : g * cross_rows + days, :] = cross[g * days : (g + 1) * days, :half]
         own_cross[g * cross_rows + days : (g + 1) * cross_rows, :] = cross[g * days : (g + 1) * days, half:]
@@ -137,9 +154,13 @@
     return pl.pallas_call(
         functools.partial(reduce_kernel, cells, grps),
         out_shape=(jax.ShapeDtypeStruct((3 * half, half), f32), jax.ShapeDtypeStruct((cross_rows, half), f32)),
-        in_specs=[pl.BlockSpec(memory_space=pltpu.VMEM)] * 2,
+        in_specs=[pl.BlockSpec(memory_space=pl.ANY)] * 2,
         out_specs=(pl.BlockSpec(memory_space=pltpu.VMEM),) * 2,
         scratch_shapes=[
+            pltpu.VMEM(sketch.shape, sketch.dtype),
+            pltpu.VMEM(slab.shape, slab.dtype),
+            dma((len(chunks_of(sketch.shape[0], SUM_STEP)),)),
+            dma((len(chunks_of(slab.shape[0], SUM_STEP)),)),
             pltpu.VMEM((3 * half, half), f32),
             pltpu.VMEM((2 * days, half), f32),
             pltpu.VMEM((grps - 1, gram_rows, half), f32),
@@ -152,6 +173,12 @@
     )(sketch, slab)
 
 
+def tree(terms):
+    while len(terms) > 1:
+        terms = [a + b for a, b in zip(terms[::2], terms[1::2])]
+    return terms[0]
+
+
 def factor(block):
     n = block.shape[0]
     shape = (SUB, n)
@@ -171,10 +198,11 @@
     for p in range(tiles):
         t, v = m[p], w[p]
         c = [col(t, p * SUB + i) for i in range(SUB)]
+        s = {(j, i): row(c[i], j) for i in range(SUB) for j in range(i + 1)}
         r_t, r_v = jnp.zeros(shape, jnp.float32), jnp.zeros(shape, jnp.float32)
         for j in range(SUB):
             at = sub == j
-            pivot = row(c[j], j)
+            pivot = s[j, j]
             inv, root = 1.0 / pivot, lax.rsqrt(pivot)
             f = jnp.where(at, -inv, c[j] * inv)
             t_j, v_j = row(t, j), row(v, j)
@@ -182,25 +210,29 @@
             r_v = jnp.where(at, v_j * root, r_v)
             t = jnp.where(at, 0.0, t) - f * t_j
             v = jnp.where(at, 0.0, v) - f * v_j
+            scaled = {i: s[j, i] * inv for i in range(j + 1, SUB)}
             for i in range(j + 1, SUB):
-                c[i] = jnp.where(at, 0.0, c[i]) - f * row(c[i], j)
+                c[i] = jnp.where(at, 0.0, c[i]) - f * s[j, i]
+                for h in range(j + 1, i + 1):
+                    s[h, i] = s[h, i] - scaled[h] * s[j, i]
         upper.append(jnp.where(lane >= sub + p * SUB, r_t, 0.0))
         inverse.append(r_v)
         if p + 1 < tiles:
             t_rows = [row(t, i) for i in range(SUB)]
             v_rows = [row(v, i) for i in range(SUB)]
             for q in range(p + 1, tiles):
-                old = m[q]
-                new, new_w = old, w[q]
-                for i in range(SUB):
-                    c_i = col(old, p * SUB + i)
-                    new = new - c_i * t_rows[i]
-                    new_w = new_w - c_i * v_rows[i]
-                m[q], w[q] = new, new_w
+                cols = [col(m[q], p * SUB + i) for i in range(SUB)]
+                m[q] = m[q] - tree([a * b for a, b in zip(cols, t_rows)])
+                w[q] = w[q] - tree([a * b for a, b in zip(cols, v_rows)])
     return jnp.concatenate(upper, axis=0), jnp.concatenate(inverse, axis=0)
 
 
-def factor_kernel(gram_ref, cross_ref, sketch_ref, r_ref, basis_ref, proj_ref, inv_ref):
+def factor_kernel(
+    gram_ref, cross_ref, sketch_hbm, r_ref, basis_hbm, proj_ref,
+    inv_ref, sketch_ref, basis_ref, load_sem, store_sems,
+):
+    load = pltpu.make_async_copy(sketch_hbm, sketch_ref, load_sem)
+    load.start()
     half = gram_ref.shape[1]
     days = cross_ref.shape[0] // 2
     r11, w11 = factor(gram_ref[0:half, :])
@@ -219,38 +251,49 @@
     inv_ref[0:half, half:] = zero
     inv_ref[half:, 0:half] = w21
     inv_ref[half:, half:] = w22
-    rows = proj_ref.shape[0]
+    rows = proj_ref.shape[1]
     mine = inv_ref[pl.ds(pl.multiple_of(lax.axis_index("cell") * rows, SUB), rows), :]
-    proj_ref[...] = dot(mine[:, :half], cross_ref[0:days, :], ((1,), (1,)), HIGHEST) + dot(
-        mine[:, half:], cross_ref[days:, :], ((1,), (1,)), HIGHEST)
+    proj_ref[...] = dot(cross_ref[0:days, :], mine[:, :half], ((1,), (1,)), HIGHEST) + dot(
+        cross_ref[days:, :], mine[:, half:], ((1,), (1,)), HIGHEST)
     whole = inv_ref[...]
     high = whole.astype(jnp.bfloat16)
     low = (whole - high.astype(jnp.float32)).astype(jnp.bfloat16)
-    total = sketch_ref.shape[0]
-    step = min(512, total)
-
-    for start in range(0, total, step):
-        part = sketch_ref[start : start + step, :]
+    load.wait()
+    stores = []
+    for rows in chunks_of(sketch_ref.shape[0], BASIS_STEP):
+        part = sketch_ref[rows, :]
         exact = dot(part, high, ((1,), (1,))) + dot(part, low, ((1,), (1,)))
-        basis_ref[start : start + step, :] = exact.astype(jnp.bfloat16)
+        basis_ref[rows, :] = exact.astype(jnp.bfloat16)
+        stores.append(pltpu.make_async_copy(basis_ref.at[rows, :], basis_hbm.at[rows, :], store_sems.at[len(stores)]))
+        stores[-1].start()
+    for store in stores:
+        store.wait()
 
 
 def local(cells, grps, sketch, slab):
     k, days = sketch.shape[1], slab.shape[1]
     blocks, cross = reduced(sketch, slab, cells, grps)
     vmem = pl.BlockSpec(memory_space=pltpu.VMEM)
-    return pl.pallas_call(
+    hbm = pl.BlockSpec(memory_space=pl.ANY)
+    r_factor, basis, projected = pl.pallas_call(
         factor_kernel,
         out_shape=(
             jax.ShapeDtypeStruct((k, k), jnp.float32),
             jax.ShapeDtypeStruct(sketch.shape, jnp.bfloat16),
-            jax.ShapeDtypeStruct((k // cells, days // grps), jnp.float32),
+            jax.ShapeDtypeStruct((days // grps, k // cells), jnp.float32),
         ),
-        in_specs=[vmem] * 3,
-        out_specs=(vmem,) * 3,
-        scratch_shapes=[pltpu.VMEM((k, k), jnp.float32)],
+        in_specs=[vmem, vmem, hbm],
+        out_specs=(vmem, hbm, vmem),
+        scratch_shapes=[
+            pltpu.VMEM((k, k), jnp.float32),
+            pltpu.VMEM(sketch.shape, jnp.bfloat16),
+            pltpu.VMEM(sketch.shape, jnp.bfloat16),
+            pltpu.SemaphoreType.DMA,
+            pltpu.SemaphoreType.DMA((len(chunks_of(sketch.shape[0], BASIS_STEP)),)),
+        ],
         name="factor_and_basis",
     )(blocks, cross, sketch)
+    return r_factor, basis, projected.T
 
 
 def solution(mesh):

time: 36.4 us -> 35.1 us (0.964)
  local copies, waits for them, and re-layouts: 1.44 us -> 0 us
    pallas_call x1 -> x0, local copies, waits for them, and re-layouts: 1.44 us -> none  [local(): pl.pallas_call(factor_kernel, out_shape=(jax.ShapeDtypeStruct((k, k), jnp...]
    pallas_call x1, Pallas kernels: 13.9 us -> 14.9 us  [local(): pl.pallas_call(factor_kernel, out_shape=(jax.ShapeDtypeStruct((k, k), jnp...]
    pallas_call x1, Pallas kernels: 20.2 us -> 19.3 us  [reduced(): pl.pallas_call(functools.partial(reduce_kernel, cells, grps), out_shape=(...]
where the time goes in v2:
time: 35.1 us; the launch traced here: 34.9 us
  Pallas kernels  34.3 us (98%)
  between operations  0.64 us (2%)
    pallas_call x1, Pallas kernels, reduced(): pl.pallas_call(functools.partial(reduce_kernel, cells, grps), out_shape=(...  19.3 us
    pallas_call x1, Pallas kernels, local(): pl.pallas_call(factor_kernel, out_shape=(jax.ShapeDtypeStruct((k, k), jnp...  14.9 us

profile of v2, /device:TPU:0, one launch (start us, length us, event | category | flops | bytes accessed | tf_op | source)
XLA Modules:
  0.0 34.9 jit_solution(73250537117714208)
XLA Ops:
  0.6 19.3 %reduce_sums.1 = (f32[384,128]{1,0:T(8,128)}, f32[64,128]{1,0:T(8,128)}) custom-call(bf16[3072,256]{1,0:T(8,128)(2,1)} %sketch_hbm.3, bf16[3072,128]{1,0:T(8,128)(2,1)} %slab_hbm.1), custom_call_target="tpu_custom_call" | custom-call | tf_op jit(solution)/shard_map/reduce_sums/pallas_call | solution.py:154
  20.0 14.9 %factor_and_basis.1 = (f32[256,256]{1,0:T(8,128)}, bf16[3072,256]{1,0:T(8,128)(2,1)}, f32[32,64]{1,0:T(8,128)}) custom-call(f32[384,128]{1,0:T(8,128)} %get-tuple-element.8.gram_ref, f32[64,128]{1,0:T(8,128)} %get-tuple-element.9.cross_ref, bf16[3072,256]{1,0:T(8,128)(2,1)} %sketch_hbm.3), custom_call_target="tpu_custom_call" | custom-call | tf_op jit(solution)/shard_map/factor_and_basis/pallas_call | solution.py:278

commit v3 on v2

--- a/solution.py
+++ b/solution.py
@@ -8,6 +8,7 @@
 from jax.sharding import PartitionSpec as P
 
 SUB = 8
+BASE = 64
 SUM_STEP = 768
 BASIS_STEP = 512
 HIGHEST = lax.Precision.HIGHEST
@@ -179,15 +180,17 @@
     return terms[0]
 
 
-def factor(block):
+def factor_base(block):
     n = block.shape[0]
-    shape = (SUB, n)
+    shape = (SUB, 2 * n)
     tiles = n // SUB
     sub = lax.broadcasted_iota(jnp.int32, shape, 0)
     lane = lax.broadcasted_iota(jnp.int32, shape, 1)
-    m = [block[q * SUB : (q + 1) * SUB, :] for q in range(tiles)]
-    w = [jnp.where(lane == sub + q * SUB, 1.0, 0.0).astype(jnp.float32) for q in range(tiles)]
-    upper, inverse = [], []
+    eye = jnp.where(
+        lax.broadcasted_iota(jnp.int32, (n, n), 0) == lax.broadcasted_iota(jnp.int32, (n, n), 1), 1.0, 0.0)
+    wide = jnp.concatenate([block, eye.astype(jnp.float32)], axis=1)
+    m = [wide[q * SUB : (q + 1) * SUB, :] for q in range(tiles)]
+    done = []
 
     def row(x, j):
         return jnp.broadcast_to(x[j : j + 1, :], shape)
@@ -196,35 +199,47 @@
         return jnp.broadcast_to(x[:, j : j + 1], shape)
 
     for p in range(tiles):
-        t, v = m[p], w[p]
+        t = m[p]
         c = [col(t, p * SUB + i) for i in range(SUB)]
         s = {(j, i): row(c[i], j) for i in range(SUB) for j in range(i + 1)}
-        r_t, r_v = jnp.zeros(shape, jnp.float32), jnp.zeros(shape, jnp.float32)
+        r = jnp.zeros(shape, jnp.float32)
         for j in range(SUB):
             at = sub == j
             pivot = s[j, j]
             inv, root = 1.0 / pivot, lax.rsqrt(pivot)
             f = jnp.where(at, -inv, c[j] * inv)
-            t_j, v_j = row(t, j), row(v, j)
-            r_t = jnp.where(at, t_j * root, r_t)
-            r_v = jnp.where(at, v_j * root, r_v)
+            t_j = row(t, j)
+            r = jnp.where(at, t_j * root, r)
             t = jnp.where(at, 0.0, t) - f * t_j
-            v = jnp.where(at, 0.0, v) - f * v_j
             scaled = {i: s[j, i] * inv for i in range(j + 1, SUB)}
             for i in range(j + 1, SUB):
                 c[i] = jnp.where(at, 0.0, c[i]) - f * s[j, i]
                 for h in range(j + 1, i + 1):
                     s[h, i] = s[h, i] - scaled[h] * s[j, i]
-        upper.append(jnp.where(lane >= sub + p * SUB, r_t, 0.0))
-        inverse.append(r_v)
+        done.append(jnp.where((lane >= sub + p * SUB), r, 0.0))
         if p + 1 < tiles:
-            t_rows = [row(t, i) for i in range(SUB)]
-            v_rows = [row(v, i) for i in range(SUB)]
+            rows = [row(t, i) for i in range(SUB)]
             for q in range(p + 1, tiles):
-                cols = [col(m[q], p * SUB + i) for i in range(SUB)]
-                m[q] = m[q] - tree([a * b for a, b in zip(cols, t_rows)])
-                w[q] = w[q] - tree([a * b for a, b in zip(cols, v_rows)])
-    return jnp.concatenate(upper, axis=0), jnp.concatenate(inverse, axis=0)
+                m[q] = m[q] - tree([col(m[q], p * SUB + i) * rows[i] for i in range(SUB)])
+    done = jnp.concatenate(done, axis=0)
+    return done[:, :n], done[:, n:]
+
+
+def factor(block):
+    n = block.shape[0]
+    if n <= BASE or n % (2 * SUB):
+        return factor_base(block)
+    h = n // 2
+    r11, w11 = factor(block[:h, :h])
+    r12 = dot(w11, block[:h, h:], ((1,), (0,)), HIGHEST)
+    r21 = r12.T
+    r22, w22 = factor(block[h:, h:] - dot(r21, r12, ((1,), (0,)), HIGHEST))
+    w21 = -dot(w22, dot(r21, w11, ((1,), (0,)), HIGHEST), ((1,), (0,)), HIGHEST)
+    zero = jnp.zeros((h, h), jnp.float32)
+    return (
+        jnp.concatenate([jnp.concatenate([r11, r12], axis=1), jnp.concatenate([zero, r22], axis=1)], axis=0),
+        jnp.concatenate([jnp.concatenate([w11, zero], axis=1), jnp.concatenate([w21, w22], axis=1)], axis=0),
+    )
 
 
 def factor_kernel(

time: 35.1 us -> 35.9 us (1.023)
  Pallas kernels: 34.3 us -> 35 us
    pallas_call x1, Pallas kernels: 14.9 us -> 15.7 us  [local(): pl.pallas_call(factor_kernel, out_shape=(jax.ShapeDtypeStruct((k, k), jnp...]
where the time goes in v3:
time: 35.9 us; the launch traced here: 35.7 us
  Pallas kernels  35 us (97%)
  between operations  0.64 us (2%)
    pallas_call x1, Pallas kernels, reduced(): pl.pallas_call(functools.partial(reduce_kernel, cells, grps), out_shape=(...  19.3 us
    pallas_call x1, Pallas kernels, local(): pl.pallas_call(factor_kernel, out_shape=(jax.ShapeDtypeStruct((k, k), jnp...  15.7 us

profile of v3, /device:TPU:0, one launch (start us, length us, event | category | flops | bytes accessed | tf_op | source)
XLA Modules:
  0.0 35.7 jit_solution(10236426317430071952)
XLA Ops:
  0.6 19.3 %reduce_sums.1 = (f32[384,128]{1,0:T(8,128)}, f32[64,128]{1,0:T(8,128)}) custom-call(bf16[3072,256]{1,0:T(8,128)(2,1)} %sketch_hbm.3, bf16[3072,128]{1,0:T(8,128)(2,1)} %slab_hbm.1), custom_call_target="tpu_custom_call" | custom-call | tf_op jit(solution)/shard_map/reduce_sums/pallas_call | solution.py:155
  20.0 15.7 %factor_and_basis.1 = (f32[256,256]{1,0:T(8,128)}, bf16[3072,256]{1,0:T(8,128)(2,1)}, f32[32,64]{1,0:T(8,128)}) custom-call(f32[384,128]{1,0:T(8,128)} %get-tuple-element.8.gram_ref, f32[64,128]{1,0:T(8,128)} %get-tuple-element.9.cross_ref, bf16[3072,256]{1,0:T(8,128)(2,1)} %sketch_hbm.3), custom_call_target="tpu_custom_call" | custom-call | tf_op jit(solution)/shard_map/factor_and_basis/pallas_call | solution.py:293

commit v4 on v3

--- a/solution.py
+++ b/solution.py
@@ -180,9 +180,10 @@
     return terms[0]
 
 
-def factor_base(block):
+def factor_base(block, ones_ref):
     n = block.shape[0]
     shape = (SUB, 2 * n)
+    ones = ones_ref[:, : 2 * n]
     tiles = n // SUB
     sub = lax.broadcasted_iota(jnp.int32, shape, 0)
     lane = lax.broadcasted_iota(jnp.int32, shape, 1)
@@ -200,7 +201,7 @@
 
     for p in range(tiles):
         t = m[p]
-        c = [col(t, p * SUB + i) for i in range(SUB)]
+        c = [col(t, p * SUB + i) * ones for i in range(SUB)]
         s = {(j, i): row(c[i], j) for i in range(SUB) for j in range(i + 1)}
         r = jnp.zeros(shape, jnp.float32)
         for j in range(SUB):
@@ -225,15 +226,15 @@
     return done[:, :n], done[:, n:]
 
 
-def factor(block):
+def factor(block, ones_ref):
     n = block.shape[0]
     if n <= BASE or n % (2 * SUB):
-        return factor_base(block)
+        return factor_base(block, ones_ref)
     h = n // 2
-    r11, w11 = factor(block[:h, :h])
+    r11, w11 = factor(block[:h, :h], ones_ref)
     r12 = dot(w11, block[:h, h:], ((1,), (0,)), HIGHEST)
     r21 = r12.T
-    r22, w22 = factor(block[h:, h:] - dot(r21, r12, ((1,), (0,)), HIGHEST))
+    r22, w22 = factor(block[h:, h:] - dot(r21, r12, ((1,), (0,)), HIGHEST), ones_ref)
     w21 = -dot(w22, dot(r21, w11, ((1,), (0,)), HIGHEST), ((1,), (0,)), HIGHEST)
     zero = jnp.zeros((h, h), jnp.float32)
     return (
@@ -244,18 +245,19 @@
 
 def factor_kernel(
     gram_ref, cross_ref, sketch_hbm, r_ref, basis_hbm, proj_ref,
-    inv_ref, sketch_ref, basis_ref, load_sem, store_sems,
+    inv_ref, ones_ref, sketch_ref, basis_ref, load_sem, store_sems,
 ):
     load = pltpu.make_async_copy(sketch_hbm, sketch_ref, load_sem)
     load.start()
+    ones_ref[...] = jnp.ones_like(ones_ref)
     half = gram_ref.shape[1]
     days = cross_ref.shape[0] // 2
-    r11, w11 = factor(gram_ref[0:half, :])
+    r11, w11 = factor(gram_ref[0:half, :], ones_ref)
     r12 = dot(w11, gram_ref[half : 2 * half, :], ((1,), (0,)), HIGHEST)
     r21 = r12.T
     rest = gram_ref[2 * half :, :] - dot(r21, r12, ((1,), (0,)), HIGHEST)
     mixed = dot(r21, w11, ((1,), (0,)), HIGHEST)
-    r22, w22 = factor(rest)
+    r22, w22 = factor(rest, ones_ref)
     w21 = -dot(w22, mixed, ((1,), (0,)), HIGHEST)
     zero = jnp.zeros((half, half), jnp.float32)
     r_ref[0:half, 0:half] = r11
@@ -301,6 +303,7 @@
         out_specs=(vmem, hbm, vmem),
         scratch_shapes=[
             pltpu.VMEM((k, k), jnp.float32),
+            pltpu.VMEM((SUB, k), jnp.float32),
             pltpu.VMEM(sketch.shape, jnp.bfloat16),
             pltpu.VMEM(sketch.shape, jnp.bfloat16),
             pltpu.SemaphoreType.DMA,

time: 35.9 us -> 33.1 us (0.922)
  Pallas kernels: 35 us -> 32.3 us
    pallas_call x1, Pallas kernels: 15.7 us -> 13 us  [local(): pl.pallas_call(factor_kernel, out_shape=(jax.ShapeDtypeStruct((k, k), jnp...]
where the time goes in v4:
time: 33.1 us; the launch traced here: 33 us
  Pallas kernels  32.3 us (98%)
  between operations  0.64 us (2%)
    pallas_call x1, Pallas kernels, reduced(): pl.pallas_call(functools.partial(reduce_kernel, cells, grps), out_shape=(...  19.3 us
    pallas_call x1, Pallas kernels, local(): pl.pallas_call(factor_kernel, out_shape=(jax.ShapeDtypeStruct((k, k), jnp...  13 us

profile of v4, /device:TPU:0, one launch (start us, length us, event | category | flops | bytes accessed | tf_op | source)
XLA Modules:
  0.0 33.0 jit_solution(12220728211408884581)
XLA Ops:
  0.6 19.3 %reduce_sums.1 = (f32[384,128]{1,0:T(8,128)}, f32[64,128]{1,0:T(8,128)}) custom-call(bf16[3072,256]{1,0:T(8,128)(2,1)} %sketch_hbm.3, bf16[3072,128]{1,0:T(8,128)(2,1)} %slab_hbm.1), custom_call_target="tpu_custom_call" | custom-call | tf_op jit(solution)/shard_map/reduce_sums/pallas_call | solution.py:155
  20.0 13.0 %factor_and_basis.1 = (f32[256,256]{1,0:T(8,128)}, bf16[3072,256]{1,0:T(8,128)(2,1)}, f32[32,64]{1,0:T(8,128)}) custom-call(f32[384,128]{1,0:T(8,128)} %get-tuple-element.8.gram_ref, f32[64,128]{1,0:T(8,128)} %get-tuple-element.9.cross_ref, bf16[3072,256]{1,0:T(8,128)(2,1)} %sketch_hbm.3), custom_call_target="tpu_custom_call" | custom-call | tf_op jit(solution)/shard_map/factor_and_basis/pallas_call | solution.py:295

commit v5 on v4

--- a/solution.py
+++ b/solution.py
@@ -220,8 +220,10 @@
         done.append(jnp.where((lane >= sub + p * SUB), r, 0.0))
         if p + 1 < tiles:
             rows = [row(t, i) for i in range(SUB)]
-            for q in range(p + 1, tiles):
-                m[q] = m[q] - tree([col(m[q], p * SUB + i) * rows[i] for i in range(SUB)])
+            later = range(p + 1, tiles)
+            terms = [[col(m[q], p * SUB + i) * rows[i] for q in later] for i in range(SUB)]
+            for at, q in enumerate(later):
+                m[q] = m[q] - tree([terms[i][at] for i in range(SUB)])
     done = jnp.concatenate(done, axis=0)
     return done[:, :n], done[:, n:]
 

time: 33.1 us -> 33.1 us (level)
  no operation moved by 1% of the time
where the time goes in v5:
time: 33.1 us; the launch traced here: 33 us
  Pallas kernels  32.3 us (98%)
  between operations  0.64 us (2%)
    pallas_call x1, Pallas kernels, reduced(): pl.pallas_call(functools.partial(reduce_kernel, cells, grps), out_shape=(...  19.3 us
    pallas_call x1, Pallas kernels, local(): pl.pallas_call(factor_kernel, out_shape=(jax.ShapeDtypeStruct((k, k), jnp...  13 us

profile of v5, /device:TPU:0, one launch (start us, length us, event | category | flops | bytes accessed | tf_op | source)
XLA Modules:
  0.0 33.0 jit_solution(12220728211408884581)
XLA Ops:
  0.6 19.3 %reduce_sums.1 = (f32[384,128]{1,0:T(8,128)}, f32[64,128]{1,0:T(8,128)}) custom-call(bf16[3072,256]{1,0:T(8,128)(2,1)} %sketch_hbm.3, bf16[3072,128]{1,0:T(8,128)(2,1)} %slab_hbm.1), custom_call_target="tpu_custom_call" | custom-call | tf_op jit(solution)/shard_map/reduce_sums/pallas_call | solution.py:155
  20.0 13.0 %factor_and_basis.1 = (f32[256,256]{1,0:T(8,128)}, bf16[3072,256]{1,0:T(8,128)(2,1)}, f32[32,64]{1,0:T(8,128)}) custom-call(f32[384,128]{1,0:T(8,128)} %get-tuple-element.8.gram_ref, f32[64,128]{1,0:T(8,128)} %get-tuple-element.9.cross_ref, bf16[3072,256]{1,0:T(8,128)(2,1)} %sketch_hbm.3), custom_call_target="tpu_custom_call" | custom-call | tf_op jit(solution)/shard_map/factor_and_basis/pallas_call | solution.py:297
